TPU v7x, 32 devices: a whole 2x2x4 slice. The times are simulated.
32 devices in a mesh: chan: 8 (over z, y), row: 2 (over core), col: 2 (over x).
Axes of the slice: x: 2, y: 2, z: 4, core: 2. Of those that a mesh axis runs over, the one named last changes fastest.
Arguments:
- volts: bfloat16 [2, 1024, 2, 52736], P(None, ('chan', 'row', 'col')), may hold values from -6 to 6
- taps: float32 [8, 512], replicated, may hold values from -2 to 2
- owner_map: int32 [24], replicated, may hold values from 0 to 15, as said below
- assign: int32 [512], replicated, may hold values from 0 to 511, each once
Outputs:
- visibility: bfloat16 [32, 2, 1024, 1024], P(('chan', 'col'), None, 'row')
Inputs may be any that keep to these rules, and one draw needn't show every extreme that they name: `owner_map`: each owner holds 1 to 2 channels, and some owner holds exactly 2. `assign`: A permutation of the stations.
All inputs are finite; a program needn't handle non-finite values.
Results may differ from a plain program's by a relative error of at most 0.0055.
Values may be sent and summed in bfloat16 or wider, within the bound.
No kernel may reach another device: no remote copies, remote signals or barrier semaphores. Data moves between devices by JAX's collectives and lax.ppermute only.
A program may use at most 192 MiB of HBM per device.

v0:
```python
import functools
import math

import jax
import jax.numpy as jnp
import numpy as np
from jax import lax
from jax.experimental import pallas as pl
from jax.experimental.pallas import tpu as pltpu
from jax.sharding import PartitionSpec as P


STATIONS = 512
NFFT = 512
TAPS = 8
BATCHES = 2
CAP = 2
LANES = 128


def slot_table(owner_map, owner_count, slot_count):
    channel_count = owner_map.shape[0]
    ranking = jnp.argsort(owner_map * channel_count + jnp.arange(channel_count, dtype=jnp.int32))
    counts = jnp.sum(
        (owner_map[None, :] == jnp.arange(owner_count, dtype=jnp.int32)[:, None]).astype(jnp.int32),
        axis=1,
    )
    starts = jnp.cumsum(counts) - counts
    slot_index = jnp.arange(slot_count, dtype=jnp.int32)
    position = jnp.clip(starts[:, None] + slot_index[None, :], 0, channel_count - 1)
    channel = jnp.take(ranking, position, axis=0)
    is_live = slot_index[None, :] < counts[:, None]
    return (channel, is_live)


def general_shards(volts, taps, owner_map, assign):
    chan_count = lax.axis_size("chan")
    rows_count = lax.axis_size("row")
    cols_count = lax.axis_size("col")
    owner_count = chan_count * cols_count
    local_inputs = volts.shape[1]
    spec_len = volts.shape[3] // NFFT - TAPS + 1
    channel, is_live = slot_table(owner_map, owner_count, CAP)
    points = jnp.arange(NFFT, dtype=jnp.int32)
    phase = (points[:, None, None] * channel.T[None, :, :] % NFFT).astype(jnp.float32) * (
        2.0 * math.pi / NFFT
    )
    weight_live = is_live.T[None, :, :].astype(jnp.float32) / math.sqrt(NFFT)
    cosine = jnp.cos(phase) * weight_live
    sine = jnp.sin(phase) * weight_live
    table = jnp.stack(
        [jnp.stack([cosine, -sine], axis=1), jnp.stack([sine, cosine], axis=1)], axis=0
    )
    total_inputs = 2 * STATIONS
    positions = jnp.arange(total_inputs, dtype=jnp.int32)
    pick = 2 * jnp.take(assign, positions // 2, axis=0) + positions % 2
    device_of = pick // local_inputs
    within = pick % local_inputs
    chan_of = device_of // (rows_count * cols_count)
    row_of = device_of // cols_count % rows_count
    col_of = device_of % cols_count
    located = ((row_of * cols_count + col_of) * chan_count + chan_of) * local_inputs + within
    row_count = total_inputs // rows_count
    row_pick = lax.dynamic_slice_in_dim(located, lax.axis_index("row") * row_count, row_count)
    total = jnp.zeros((CAP, 2 * row_count, total_inputs), jnp.float32)
    for batch in range(BATCHES):
        signal = (
            volts[batch].astype(jnp.float32).reshape(local_inputs, 2, spec_len + TAPS - 1, NFFT)
        )
        summed = jnp.zeros((local_inputs, 2, spec_len, NFFT), jnp.float32)
        for tap_index in range(TAPS):
            summed = (
                summed
                + taps[tap_index][None, None, None, :]
                * signal[:, :, tap_index : tap_index + spec_len, :]
            )
        result = jnp.einsum("iasj,ajbkg->kgibs", summed, table, precision=lax.Precision.HIGHEST)
        turned = lax.all_to_all(
            lax.all_to_all(
                result.reshape(CAP, chan_count, cols_count, local_inputs, 2 * spec_len).astype(
                    jnp.bfloat16
                ),
                "chan",
                split_axis=1,
                concat_axis=3,
                tiled=True,
            ),
            "col",
            split_axis=2,
            concat_axis=3,
            tiled=True,
        )
        gathered = lax.all_gather(turned, "row", axis=3, tiled=True)
        flat = gathered.reshape(CAP, total_inputs, -1)
        width = flat.shape[2]
        rows = jnp.take(flat, row_pick, axis=1)
        split_rows = rows.reshape(CAP, row_count, width // (2 * spec_len), 2, spec_len)
        flipped = jnp.stack(
            [split_rows[:, :, :, 1, :], -split_rows[:, :, :, 0, :]], axis=3
        ).reshape(CAP, row_count, width)
        stacked = jnp.concatenate([rows, flipped], axis=1)
        columns = jnp.take(flat, located, axis=1)
        total = total + jnp.einsum(
            "kpx,kqx->kpq", stacked, columns, preferred_element_type=jnp.float32
        )
    scale = 1.0 / math.sqrt(2 * BATCHES * spec_len)
    return (total * scale).reshape(CAP, 2, row_count, total_inputs).astype(jnp.bfloat16)


def trig_table(channels):
    points = np.arange(NFFT)
    phase = (np.arange(channels)[:, None] * points[None, :] % NFFT) * (2.0 * math.pi / NFFT)
    unit = 1.0 / math.sqrt(NFFT)
    return np.concatenate([np.cos(phase), np.sin(phase)], axis=0).astype(np.float32) * np.float32(unit)


BLOCK = 4
MXU = 256
UNROLL = 2
UNIT = 16
ORDER = (0, 1, 2, 2, 0, 1, 2, 2)
WHOLE = ((0, (0, 1, 2)), (1, (3,)), (2, (4, 5, 6)), (3, (7,)))
HALF = ((1, (0, 1)), (3, (4, 5)))
LAG = 8


def spectra_kernel(segments, channels, owners, columns, inputs, rows,
                   owner_hbm, volts_ref, taps_hbm, trig_hbm, out_ref,
                   wave, weight, prod, lined, taps_ref, trig_ref,
                   owner_ref, count, table, sem, small):
    blocks = wave.shape[0]
    sets = blocks // UNROLL
    rounds = (sets - 3) // 2
    halves = 2 * channels
    stride = lined.shape[0] // channels
    lanes = 2 * inputs

    loads = [
        pltpu.make_async_copy(taps_hbm, taps_ref, small.at[0]),
        pltpu.make_async_copy(trig_hbm, trig_ref, small.at[1]),
        pltpu.make_async_copy(owner_hbm, owner_ref, small.at[2]),
    ]
    for load in loads:
        load.start()

    units = []
    fetches = []
    for batch, first_row, spectra_count in segments:
        source = volts_ref.at[batch].reshape(lanes, volts_ref.shape[3])
        for u in range(spectra_count // (2 * UNIT)):
            units.append(2 * len(fetches) + u * UNIT)
        for block in range(-(-(spectra_count + TAPS - 1) // BLOCK)):
            fetches.append((source, first_row + block * BLOCK))

    def fetch(block):
        source, row = fetches[block]
        whole = min(BLOCK, rows - row)
        pieces = [(0, row, whole)] + [(step, rows - 1, 1) for step in range(whole, BLOCK)]
        for step, start, held in pieces:
            pltpu.make_async_copy(
                source.at[:, start * NFFT:(start + held) * NFFT],
                wave.at[block, :, step * NFFT:(step + held) * NFFT],
                sem.at[block],
            ).start()

    for block in range(blocks):
        fetch(block)

    for load in loads:
        load.wait()

    for tap in range(TAPS):
        scaled = trig_ref[...] * taps_ref[tap:tap + 1, :]
        high = scaled.astype(jnp.bfloat16)
        low = (scaled - high.astype(jnp.float32)).astype(jnp.bfloat16)
        weight[tap * halves:(tap + 1) * halves, :NFFT] = high
        weight[tap * halves:(tap + 1) * halves, NFFT:] = low

    for owner in range(owners):
        count[owner] = 0
        for slot in range(CAP):
            table[owner * CAP + slot] = 0
    table[owners * CAP] = 0

    lane = lax.broadcasted_iota(jnp.int32, (halves, LANES), 1)
    low_half = lane < LANES // 2
    even = (lax.broadcasted_iota(jnp.int32, (channels, LANES), 1) % 2) == 0

    def tap_sum(tile, odd):
        total = prod[tile, odd * halves:(odd + 1) * halves, :]
        for e in range(1, TAPS // 2):
            m = 2 * e + odd
            total = total + prod[tile + e, m * halves:(m + 1) * halves, :]
        return total

    def finish(pair, turned):
        for step in range(2 * UNROLL):
            tile = pair + step
            following = pltpu.roll(tap_sum(tile + 1, 1), LANES // 2, 1)
            value = tap_sum(tile, 0) + jnp.where(low_half, turned, following)
            turned = following
            cosine = value[:channels]
            sine = value[channels:]
            mixed = cosine + jnp.where(
                even, pltpu.roll(sine, LANES - 1, 1), -pltpu.roll(sine, 1, 1)
            )
            lined[pl.ds(tile, channels, stride=stride), :] = mixed
        return turned

    def place(k):
        real = k < channels
        owner = owner_ref[jnp.minimum(k, channels - 1)]
        used = count[owner]
        table[jnp.where(real, owner * CAP + used, owners * CAP)] = k
        count[owner] = jnp.where(real, used + 1, used)

    def wait(first):
        for step in range(UNROLL):
            pltpu.make_async_copy(wave.at[first + step], wave.at[first + step], sem.at[first + step]).wait()

    def stage(first, part):
        for step in range(UNROLL):
            x = [
                wave[first + step, :, row * NFFT + part * MXU:row * NFFT + (part + 1) * MXU]
                for row in range(BLOCK)
            ]
            pltpu.matmul_push_rhs(jnp.concatenate(x, axis=0), part, step, transpose=True)

    def multiply(totals, following):
        for part in range(NFFT // MXU):
            for total in totals:
                pltpu.matmul_acc_lhs(
                    total, weight[:, part * MXU:(part + 1) * MXU], load_staged_rhs=part
                )
            if following is not None:
                stage(following, part)
            for total in totals:
                pltpu.matmul_acc_lhs(
                    total, weight[:, NFFT + part * MXU:NFFT + (part + 1) * MXU]
                )

    def collect(first, totals):
        for step, total in enumerate(totals):
            y = pltpu.matmul_pop(total)
            prod[2 * (first + step) + LAG] = y[:, :LANES]
            prod[2 * (first + step) + LAG + 1] = y[:, LANES:]

    def run(*totals):
        even_totals = totals[:2]
        odd_totals = totals[2:]

        share = pl.cdiv(channels, rounds)

        def body(group, turned):
            first = group * 2 * UNROLL
            wait(first + 2 * UNROLL)
            wait(first + 3 * UNROLL)
            for extra in range(share):
                place(group * share + extra)
            multiply(odd_totals, first + 2 * UNROLL)
            turned = finish(2 * first + LAG - 4 - 2 * UNROLL, turned)
            collect(first, even_totals)
            multiply(even_totals, first + 3 * UNROLL)
            turned = finish(2 * first + LAG - 4, turned)
            collect(first + UNROLL, odd_totals)
            return turned

        wait(0)
        wait(UNROLL)
        for part in range(NFFT // MXU):
            stage(0, part)
        multiply(even_totals, UNROLL)
        turned = lax.fori_loop(0, rounds, body, jnp.zeros((halves, LANES), jnp.float32))
        for index in range(2 * rounds + 1, sets):
            if index + 1 < sets:
                wait((index + 1) * UNROLL)
            multiply(
                (even_totals, odd_totals)[index % 2],
                (index + 1) * UNROLL if index + 1 < sets else None,
            )
            turned = finish(4 * (index - 1) + LAG - 8, turned)
            collect((index - 1) * UNROLL, (even_totals, odd_totals)[1 - index % 2])
        turned = finish(4 * (sets - 1) + LAG - 8, turned)
        collect((sets - 1) * UNROLL, (even_totals, odd_totals)[(sets - 1) % 2])
        finish(4 * sets + LAG - 8, turned)

    shape = (TAPS * halves, MXU)
    pl.run_scoped(run, *(pltpu.ACC(mxu_id=index % 2)(shape, jnp.float32) for index in range(4)))

    stations = inputs // 2
    to = lax.broadcasted_iota(jnp.int32, (2 * LANES, MXU), 0)
    at = lax.broadcasted_iota(jnp.int32, (2 * LANES, MXU), 1)
    row = to % LANES
    quarter = row // stations % 4
    origin = (
        quarter % 2 * lanes + (row % stations * 2 + row // (4 * stations)) * 2 + quarter // 2
        + to - row
    )
    turn = (at == origin).astype(jnp.bfloat16)
    spot = lax.broadcasted_iota(jnp.int32, (stations, LANES), 1) // UNIT
    shared = spot % 4 < 2

    def pick(choices, dealt):
        value = None
        for quarter, spots in choices:
            piece = dealt[quarter * stations:(quarter + 1) * stations]
            if value is None:
                value = piece
            else:
                inside = functools.reduce(jnp.logical_or, [spot == u for u in spots])
                value = jnp.where(inside, piece, value)
        return value

    def deal(*totals):
        for pair in range(owners // 2):
            total = totals[pair % len(totals)]
            sides = []
            for side in range(2):
                owner = 2 * pair + side
                pieces = []
                for slot in range(CAP):
                    first = table[owner * CAP + slot] * stride + LAG
                    for unit in ORDER:
                        start = pl.multiple_of(first + units[unit], 8)
                        pieces.append(lined[pl.ds(start, UNIT), :].astype(jnp.bfloat16))
                sides.append(jnp.concatenate(pieces, axis=0))
            pltpu.matmul_push_rhs(
                jnp.concatenate(sides, axis=1), pair // 2 % 2, pair % 2, transpose=True
            )
            pltpu.matmul_acc_lhs(total, turn, load_staged_rhs=pair // 2 % 2)
            dealt = pltpu.matmul_pop(total)
            for side in range(2):
                owner = 2 * pair + side
                for slot in range(CAP):
                    tile = dealt[side * LANES:(side + 1) * LANES, slot * LANES:(slot + 1) * LANES]
                    pols = (tile[:LANES // 2], tile[LANES // 2:])
                    moved = pltpu.roll(pick(HALF, pols[1]), 2 * UNIT, 1)
                    value = jnp.concatenate(
                        [
                            pick(WHOLE, pols[0]),
                            jnp.where(shared, pick(HALF, pols[0]), moved),
                            pick(WHOLE, pols[1]),
                        ],
                        axis=1,
                    )
                    target = (owner // columns * CAP + slot) * columns + owner % columns
                    out_ref[target] = value.astype(jnp.bfloat16)

    pl.run_scoped(
        deal, *(pltpu.ACC(mxu_id=index % 2)((2 * LANES, MXU), jnp.float32) for index in range(4))
    )


def spectra(segments, volts, taps, owner_map, owners, columns):
    channels = owner_map.shape[0]
    inputs = volts.shape[1]
    rows = volts.shape[3] // NFFT
    count = sum(segment[2] for segment in segments)
    blocks = sum(-(-(segment[2] + TAPS - 1) // BLOCK) for segment in segments)
    halves = 2 * channels
    stride = 2 * blocks + LAG
    stride = -(-stride // 8) * 8
    trig = jnp.asarray(trig_table(channels))
    hbm = pl.BlockSpec(memory_space=pltpu.HBM)
    return pl.pallas_call(
        functools.partial(spectra_kernel, segments, channels, owners, columns, inputs, rows),
        out_shape=jax.ShapeDtypeStruct((owners * CAP, inputs // 2, 4 * count), jnp.bfloat16),
        in_specs=[hbm] * 4,
        out_specs=pl.BlockSpec(memory_space=pltpu.VMEM),
        scratch_shapes=[
            pltpu.VMEM((blocks, inputs * 2, BLOCK * NFFT), jnp.bfloat16),
            pltpu.VMEM((TAPS * halves, 2 * NFFT), jnp.bfloat16),
            pltpu.VMEM((2 * blocks + LAG, TAPS * halves, LANES), jnp.float32),
            pltpu.VMEM((channels * stride, LANES), jnp.float32),
            pltpu.VMEM(taps.shape, jnp.float32),
            pltpu.VMEM(trig.shape, jnp.float32),
            pltpu.SMEM((channels,), jnp.int32),
            pltpu.SMEM((owners,), jnp.int32),
            pltpu.SMEM((owners * CAP + 1,), jnp.int32),
            pltpu.SemaphoreType.DMA((blocks,)),
            pltpu.SemaphoreType.DMA((3,)),
        ],
        compiler_params=pltpu.CompilerParams(vmem_limit_bytes=48 * 1024 * 1024),
        cost_estimate=pl.CostEstimate(
            flops=4 * blocks * BLOCK * inputs * 2 * NFFT * TAPS * halves,
            bytes_accessed=blocks * BLOCK * inputs * 4 * NFFT, transcendentals=0
        ),
        name="spectra",
    )(*(pltpu.with_memory_space_constraint(x, pltpu.HBM) for x in (owner_map, volts, taps, trig)))


def order_kernel(place_ref, got_ref, cols_ref):
    half = got_ref.shape[0]
    total = 2 * half
    second = pltpu.roll(
        got_ref[:, LANES:2 * LANES].astype(jnp.float32), LANES - 2 * UNIT, 1
    ).astype(jnp.bfloat16)

    def run(*totals):
        for k in range(total // MXU):
            at = slice(k * MXU % half, k * MXU % half + MXU)
            if k * MXU < half:
                right = got_ref[at, :2 * LANES]
            else:
                right = jnp.concatenate([got_ref[at, 2 * LANES:], second[at]], axis=1)
            for unit in range(2):
                pltpu.matmul_push_rhs(right, k % 2, unit)
                pltpu.matmul_acc_lhs(
                    totals[unit],
                    place_ref[unit * half:(unit + 1) * half, k * MXU:(k + 1) * MXU],
                    load_staged_rhs=k % 2,
                )
        for unit in range(2):
            cols_ref[unit * half:(unit + 1) * half] = pltpu.matmul_pop(totals[unit]).astype(
                jnp.bfloat16
            )

    pl.run_scoped(run, *(pltpu.ACC(mxu_id=unit)((half, MXU), jnp.float32) for unit in range(2)))


def order(place, got):
    half = got.shape[0]
    vmem = pl.BlockSpec(memory_space=pltpu.VMEM)
    return pl.pallas_call(
        order_kernel,
        out_shape=jax.ShapeDtypeStruct((2 * half, MXU), jnp.bfloat16),
        in_specs=[vmem] * 2,
        out_specs=vmem,
        compiler_params=pltpu.CompilerParams(vmem_limit_bytes=16 * 1024 * 1024),
        cost_estimate=pl.CostEstimate(
            flops=8 * half * half * MXU, bytes_accessed=8 * half * half, transcendentals=0
        ),
        name="order",
    )(place, got)


def visibility_kernel(scale, mine, row_count, owner_ref, cols_a, cols_b, *rest):
    total = cols_a.shape[0]
    steps = total // MXU
    if mine:
        far, made, near, lead_a, lead_b, sem = rest
        bring = pltpu.make_async_copy(far, near, sem.at[0])
        bring.start()
    else:
        ready, out_hbm, made, lead_a, lead_b, sem = rest
    my_row = lax.axis_index("row")
    slot = my_row if mine else 1 - my_row

    def copy(source, target, step, number):
        return pltpu.make_async_copy(
            source.at[step], out_hbm.at[target, :, :, step * MXU:(step + 1) * MXU], sem.at[number]
        )

    if not mine:
        for step in range(steps):
            copy(ready, my_row, step, step).start()

    first = pl.multiple_of(my_row * row_count, row_count)
    lane = lax.broadcasted_iota(jnp.int32, (row_count, LANES), 1)
    front = lane < LANES // 2
    shared = lane % (LANES // 2) < 2 * UNIT

    for cols, lead in ((cols_a, lead_a), (cols_b, lead_b)):
        for t in range(MXU // LANES):
            at = slice(t * LANES, (t + 1) * LANES)
            own = cols[pl.ds(first, row_count), at].astype(jnp.float32)
            if t == 1:
                own = jnp.where(shared, own, 0.0)
            turned = pltpu.roll(own, LANES // 2, 1)
            lead[0, :, at] = own.astype(jnp.bfloat16)
            lead[1, :, at] = jnp.where(front, turned, -turned).astype(jnp.bfloat16)

    me = lax.axis_index("chan") * lax.axis_size("col") + lax.axis_index("col")
    owned = jnp.int32(0)
    for k in range(owner_ref.shape[0]):
        owned = owned + jnp.where(owner_ref[k] == me, 1, 0)
    factor = jnp.where(slot < owned, jnp.float32(scale), jnp.float32(0.0))

    def run(*totals):
        def flush(step):
            for unit in range(2):
                value = pltpu.matmul_pop(totals[2 * unit + step % 2]) * factor
                made[step, unit] = value.astype(jnp.bfloat16)
            if not mine:
                copy(made, slot, step, steps + step).start()

        for step in range(steps):
            for turn, (cols, lead) in enumerate(((cols_a, lead_a), (cols_b, lead_b))):
                for unit in range(2):
                    pltpu.matmul_push_rhs(
                        cols[step * MXU:(step + 1) * MXU, :], turn, unit, transpose=True
                    )
                    pltpu.matmul_acc_lhs(
                        totals[2 * unit + step % 2], lead[unit], load_staged_rhs=turn
                    )
            if step > 0:
                flush(step - 1)
        flush(steps - 1)

    shape = (row_count, MXU)
    pl.run_scoped(run, *(pltpu.ACC(mxu_id=index // 2)(shape, jnp.float32) for index in range(4)))
    if mine:
        bring.wait()
    else:
        for step in range(steps):
            copy(ready, my_row, step, step).wait()
            copy(made, slot, step, steps + step).wait()


def visibility(scale, owner_map, cols_a, cols_b, row_count, far=None, ready=None):
    total, width = cols_a.shape
    steps = total // MXU
    vmem = pl.BlockSpec(memory_space=pltpu.VMEM)
    hbm = pl.BlockSpec(memory_space=pltpu.HBM)
    kept = (steps, 2, row_count, MXU)
    scratch = [pltpu.VMEM((2, row_count, MXU), jnp.bfloat16)] * 2
    scratch.append(pltpu.SemaphoreType.DMA((2 * steps,)))
    if ready is None:
        more, more_spec = (far,), [hbm]
        out_shape = [jax.ShapeDtypeStruct(shape, jnp.bfloat16) for shape in (kept, (total, width))]
        out_specs = [vmem, vmem]
    else:
        more, more_spec = (ready,), [vmem]
        out_shape = jax.ShapeDtypeStruct((CAP, 2, row_count, total), jnp.bfloat16)
        out_specs = hbm
        scratch.insert(0, pltpu.VMEM(kept, jnp.bfloat16))
    return pl.pallas_call(
        functools.partial(visibility_kernel, scale, ready is None, row_count),
        out_shape=out_shape,
        in_specs=[pl.BlockSpec(memory_space=pltpu.SMEM), vmem, vmem, *more_spec],
        out_specs=out_specs,
        scratch_shapes=scratch,
        compiler_params=pltpu.CompilerParams(vmem_limit_bytes=24 * 1024 * 1024),
        cost_estimate=pl.CostEstimate(
            flops=8 * row_count * total * MXU, bytes_accessed=8 * row_count * total,
            transcendentals=0,
        ),
        name="visibility",
    )(owner_map, cols_a, cols_b, *more)


def tiled_shards(volts, taps, owner_map, assign):
    chan_count = lax.axis_size("chan")
    rows_count = lax.axis_size("row")
    cols_count = lax.axis_size("col")
    owners = chan_count * cols_count
    spec_len = volts.shape[3] // NFFT - TAPS + 1
    total_inputs = 2 * STATIONS
    row_count = total_inputs // rows_count
    positions = jnp.arange(total_inputs, dtype=jnp.int32)
    wanted = positions % 2 * STATIONS + jnp.repeat(assign, 2)
    place = (wanted[:, None] == positions[None, :]).astype(jnp.bfloat16)
    swap = [(0, 1), (1, 0)]
    scale = 1.0 / math.sqrt(2 * BATCHES * spec_len)
    own = []
    other = []
    owner_now = owner_map
    for batch in range(2):
        chunk = ((batch, 0, spec_len),)
        sent = spectra(chunk, volts, taps, owner_now, owners, cols_count)
        owner_now, sent = lax.optimization_barrier((owner_now, sent))
        turned = lax.all_to_all(
            sent, ("chan", "row", "col"), split_axis=0, concat_axis=0, tiled=True
        )
        own.append(order(place, turned.reshape(total_inputs // 2, -1)))
        other.append(lax.ppermute(own[-1], "row", swap))
    ready, near = visibility(scale, owner_map, own[0], own[1], row_count, far=other[0])
    return visibility(scale, owner_map, near, other[1], row_count, ready=ready)


def fits(volts, owner_map, mesh):
    rows = volts.shape[3] // NFFT
    return (
        4 * volts.shape[1] == LANES
        and mesh.shape["row"] == CAP == 2
        and rows - TAPS + 1 == 6 * UNIT
        and owner_map.shape[0] % 8 == 0
        and TAPS * 2 * owner_map.shape[0] <= 384
    )


def solution(mesh):
    placed = (P(None, ("chan", "row", "col"), None, None), P(), P(), P())

    def shards(volts, taps, owner_map, assign):
        if fits(volts, owner_map, mesh):
            return tiled_shards(volts, taps, owner_map, assign)
        return general_shards(volts, taps, owner_map, assign)

    return jax.shard_map(
        shards,
        mesh=mesh,
        in_specs=placed,
        out_specs=P(("chan", "col"), None, "row", None),
        check_vma=False,
    )
```

profile of v0, /device:TPU:0, one launch (start us, length us, event | category | flops | bytes accessed | tf_op | source)
XLA Modules:
  0.0 51.0 jit_solution(15860426927349197612)
XLA Ops:
  0.0 8.8 %spectra.2 = bf16[32,16,384]{2,1,0:T(8,128)(2,1)} custom-call(s32[24]{0:T(128)} %owner_ref.3, bf16[2,32,2,52736]{3,2,1,0:T(2,128)(2,1)} %volts_ref.3, f32[8,512]{1,0:T(8,128)} %taps_hbm.3, f32[48,512]{1,0:T(8,128)} %constant.20.clone.trig_hbm), custom_call_target="tpu_custom_call" | custom-call | flops 5234491392 | bytes 6815744 | tf_op jit(solution)/shard_map/spectra/pallas_call | solution.py:365
  8.8 7.3 %all-to-all-start = ((bf16[32,16,384]{2,1,0:T(8,128)(2,1)}), bf16[32,16,384]{2,1,0:T(8,128)(2,1)S(1)}, u32[]{:S(2)}, u32[]{:S(2)}) async-start(bf16[32,16,384]{2,1,0:T(8,128)(2,1)} %spectra.2), calls=%async_computation | async-start | bytes 786432 | tf_op jit(solution)/shard_map/all_to_all | solution.py:562
  16.2 0.0 copy-start.1
  16.2 8.9 %spectra.3 = bf16[32,16,384]{2,1,0:T(8,128)(2,1)} custom-call(s32[24]{0:T(128)} %owner_ref.3, bf16[2,32,2,52736]{3,2,1,0:T(2,128)(2,1)} %volts_ref.3, f32[8,512]{1,0:T(8,128)} %taps_hbm.3, f32[48,512]{1,0:T(8,128)} %constant.20.clone.trig_hbm), custom_call_target="tpu_custom_call" | custom-call | flops 5234491392 | bytes 6815744 | tf_op jit(solution)/shard_map/spectra/pallas_call | solution.py:365
  25.1 3.8 %all-to-all-done = bf16[32,16,384]{2,1,0:T(8,128)(2,1)S(1)} async-done(((bf16[32,16,384]{2,1,0:T(8,128)(2,1)}), bf16[32,16,384]{2,1,0:T(8,128)(2,1)S(1)}, u32[]{:S(2)}, u32[]{:S(2)}) %all-to-all-start) | async-done | bytes 393248 | tf_op jit(solution)/shard_map/all_to_all | solution.py:562
  28.9 3.1 %all-to-all-start.1 = ((bf16[32,16,384]{2,1,0:T(8,128)(2,1)}), bf16[32,16,384]{2,1,0:T(8,128)(2,1)S(1)}, u32[]{:S(2)}, u32[]{:S(2)}) async-start(bf16[32,16,384]{2,1,0:T(8,128)(2,1)} %spectra.3), calls=%async_computation.1 | async-start | bytes 786432 | tf_op jit(solution)/shard_map/all_to_all | solution.py:562
  32.0 0.0 copy-done.1
  32.0 0.1 broadcast_in_dim.2
  32.1 0.0 copy-start
  32.1 0.2 reshape.24
  32.3 0.4 fusion.place_ref
  32.7 0.7 %order.2.cols_a = bf16[1024,256]{1,0:T(8,128)(2,1)S(1)} custom-call(bf16[1024,1024]{1,0:T(8,128)(2,1)S(1)} %fusion.place_ref, bf16[512,384]{1,0:T(8,128)(2,1)S(1)} %bitcast.2), custom_call_target="tpu_custom_call" | custom-call | flops 536870912 | bytes 2097152 | tf_op jit(solution)/shard_map/order/pallas_call | solution.py:424
  33.4 0.3 collective-permute-start
  33.8 11.0 %all-to-all-done.1 = bf16[32,16,384]{2,1,0:T(8,128)(2,1)S(1)} async-done(((bf16[32,16,384]{2,1,0:T(8,128)(2,1)}), bf16[32,16,384]{2,1,0:T(8,128)(2,1)S(1)}, u32[]{:S(2)}, u32[]{:S(2)}) %all-to-all-start.1) | async-done | bytes 393248 | tf_op jit(solution)/shard_map/all_to_all | solution.py:562
  44.7 0.7 %order.3.cols_b = bf16[1024,256]{1,0:T(8,128)(2,1)S(1)} custom-call(bf16[1024,1024]{1,0:T(8,128)(2,1)S(1)} %fusion.place_ref, bf16[512,384]{1,0:T(8,128)(2,1)S(1)} %bitcast.3), custom_call_target="tpu_custom_call" | custom-call | flops 536870912 | bytes 2097152 | tf_op jit(solution)/shard_map/order/pallas_call | solution.py:424
  45.4 0.8 %collective-permute-start.1 = (bf16[1024,256]{1,0:T(8,128)(2,1)S(1)}, bf16[1024,256]{1,0:T(8,128)(2,1)S(1)}, u32[]{:S(2)}, u32[]{:S(2)}) collective-permute-start(bf16[1024,256]{1,0:T(8,128)(2,1)S(1)} %order.3.cols_b), channel_id=1, source_target_pairs={{0,2},{2,0},{1,3},{3,1},{4,6},{6,4},{5,7},{7,5},{8,10},{10,8},{9,1... | collective-permute-start | bytes 1572872 | tf_op jit(solution)/shard_map/ppermute | solution.py:566
  46.2 0.0 collective-permute-done.rest_0_
  46.2 0.0 copy-done
  46.2 1.9 %visibility.2 = (bf16[4,2,512,256]{3,2,1,0:T(8,128)(2,1)S(1)}, bf16[1024,256]{1,0:T(8,128)(2,1)S(1)}) custom-call(s32[24]{0:T(128)S(1)} %copy-done, bf16[1024,256]{1,0:T(8,128)(2,1)S(1)} %order.2.cols_a, bf16[1024,256]{1,0:T(8,128)(2,1)S(1)} %order.3.cols_b, bf16[1024,256]{1,0:T(8,128)(2,1)} %collective-permute-done.rest_0_), custom_call_target="tpu_custom_call" | custom-call | flops 1073741824 | bytes 4194304 | tf_op jit(solution)/shard_map/visibility/pallas_call | solution.py:527
  48.1 0.0 collective-permute-done.1.cols_b
  48.1 2.9 %visibility.3 = bf16[2,2,512,1024]{3,2,1,0:T(8,128)(2,1)} custom-call(s32[24]{0:T(128)S(1)} %copy-done, bf16[1024,256]{1,0:T(8,128)(2,1)S(1)} %get-tuple-element.13.cols_a, bf16[1024,256]{1,0:T(8,128)(2,1)S(1)} %collective-permute-done.1.cols_b, bf16[4,2,512,256]{3,2,1,0:T(8,128)(2,1)S(1)} %get-tuple-element.14.rest_0_), custom_call_target="tpu_custom_call" | custom-call | flops 1073741824 | bytes 4194304 | tf_op jit(solution)/shard_map/visibility/pallas_call | solution.py:527
  (1 shorter events, 0.0 us)
Async XLA Ops:
  8.8 20.1 %all-to-all-start = ((bf16[32,16,384]{2,1,0:T(8,128)(2,1)}), bf16[32,16,384]{2,1,0:T(8,128)(2,1)S(1)}, u32[]{:S(2)}, u32[]{:S(2)}) async-start(bf16[32,16,384]{2,1,0:T(8,128)(2,1)} %spectra.2), calls=%async_computation | async-start | bytes 786432 | tf_op jit(solution)/shard_map/all_to_all | solution.py:562
  16.2 15.8 %copy-start.1 = (s32[512]{0:T(512)S(1)}, s32[512]{0:T(512)}, u32[]{:S(2)}) copy-start(s32[512]{0:T(512)} %param.9) | copy-start | bytes 6148
  28.9 15.8 %all-to-all-start.1 = ((bf16[32,16,384]{2,1,0:T(8,128)(2,1)}), bf16[32,16,384]{2,1,0:T(8,128)(2,1)S(1)}, u32[]{:S(2)}, u32[]{:S(2)}) async-start(bf16[32,16,384]{2,1,0:T(8,128)(2,1)} %spectra.3), calls=%async_computation.1 | async-start | bytes 786432 | tf_op jit(solution)/shard_map/all_to_all | solution.py:562
  32.1 14.1 %copy-start = (s32[24]{0:T(128)S(1)}, s32[24]{0:T(128)}, u32[]{:S(2)}) copy-start(s32[24]{0:T(128)} %owner_ref.3) | copy-start | bytes 292
  33.4 12.7 %collective-permute-start = (bf16[1024,256]{1,0:T(8,128)(2,1)S(1)}, bf16[1024,256]{1,0:T(8,128)(2,1)}, u32[]{:S(2)}, u32[]{:S(2)}) collective-permute-start(bf16[1024,256]{1,0:T(8,128)(2,1)S(1)} %order.2.cols_a), channel_id=1, source_target_pairs={{0,2},{2,0},{1,3},{3,1},{4,6},{6,4},{5,7},{7,5},{8,10},{10,8},{9,1... | collective-permute-start | bytes 1572872 | tf_op jit(solution)/shard_map/ppermute | solution.py:566
  45.4 2.7 %collective-permute-start.1 = (bf16[1024,256]{1,0:T(8,128)(2,1)S(1)}, bf16[1024,256]{1,0:T(8,128)(2,1)S(1)}, u32[]{:S(2)}, u32[]{:S(2)}) collective-permute-start(bf16[1024,256]{1,0:T(8,128)(2,1)S(1)} %order.3.cols_b), channel_id=1, source_target_pairs={{0,2},{2,0},{1,3},{3,1},{4,6},{6,4},{5,7},{7,5},{8,10},{10,8},{9,1... | collective-permute-start | bytes 1572872 | tf_op jit(solution)/shard_map/ppermute | solution.py:566
where the time goes:
time: 51.5 us; the launch traced here: 51 us
  Pallas kernels  23.9 us (46%)
  waiting for transfers between devices  14.8 us (29%)
  starting transfers between devices  11.5 us (22%)
    pallas_call x2, Pallas kernels, spectra(): pl.pallas_call(functools.partial(spectra_kernel, segments, channels, owne...  17.7 us
    all_to_all x2, waiting for transfers between devices, tiled_shards(): lax.all_to_all(sent, ('chan', 'row', 'col'), split_axis=0, concat_axis=0,...  14.8 us
    all_to_all x2, starting transfers between devices, tiled_shards(): lax.all_to_all(sent, ('chan', 'row', 'col'), split_axis=0, concat_axis=0,...  10.4 us
    pallas_call x2, Pallas kernels, visibility(): pl.pallas_call(functools.partial(visibility_kernel, scale, ready is None,...  4.81 us
    pallas_call x2, Pallas kernels, order(): pl.pallas_call(order_kernel, out_shape=jax.ShapeDtypeStruct((2 * half, MX...  1.41 us
    ppermute x2, starting transfers between devices, tiled_shards(): other.append(lax.ppermute(own[-1], 'row', swap))  1.07 us
  transfers between devices with their start and end apart: 4, of which 2 were waited for; matrix products, arithmetic and copies ran while one was open for 1% of the time, Pallas kernels for 24%

commit v1 on v0

--- a/solution.py
+++ b/solution.py
@@ -126,8 +126,8 @@
 
 def spectra_kernel(segments, channels, owners, columns, inputs, rows,
                    owner_hbm, volts_ref, taps_hbm, trig_hbm, out_ref,
-                   wave, weight, prod, lined, taps_ref, trig_ref,
-                   owner_ref, count, table, sem, small):
+                   wave, weight, prod, lined, turn_ref, taps_ref, trig_ref,
+                   owner_ref, count, table, made, sem, small, gone):
     blocks = wave.shape[0]
     sets = blocks // UNROLL
     rounds = (sets - 3) // 2
@@ -165,6 +165,17 @@
 
     for block in range(blocks):
         fetch(block)
+
+    stations = inputs // 2
+    to = lax.broadcasted_iota(jnp.int32, (2 * LANES, MXU), 0)
+    at = lax.broadcasted_iota(jnp.int32, (2 * LANES, MXU), 1)
+    row = to % LANES
+    quarter = row // stations % 4
+    origin = (
+        quarter % 2 * lanes + (row % stations * 2 + row // (4 * stations)) * 2 + quarter // 2
+        + to - row
+    )
+    turn_ref[...] = (at == origin).astype(jnp.bfloat16)
 
     for load in loads:
         load.wait()
@@ -287,16 +298,6 @@
     shape = (TAPS * halves, MXU)
     pl.run_scoped(run, *(pltpu.ACC(mxu_id=index % 2)(shape, jnp.float32) for index in range(4)))
 
-    stations = inputs // 2
-    to = lax.broadcasted_iota(jnp.int32, (2 * LANES, MXU), 0)
-    at = lax.broadcasted_iota(jnp.int32, (2 * LANES, MXU), 1)
-    row = to % LANES
-    quarter = row // stations % 4
-    origin = (
-        quarter % 2 * lanes + (row % stations * 2 + row // (4 * stations)) * 2 + quarter // 2
-        + to - row
-    )
-    turn = (at == origin).astype(jnp.bfloat16)
     spot = lax.broadcasted_iota(jnp.int32, (stations, LANES), 1) // UNIT
     shared = spot % 4 < 2
 
@@ -310,6 +311,10 @@
                 inside = functools.reduce(jnp.logical_or, [spot == u for u in spots])
                 value = jnp.where(inside, piece, value)
         return value
+
+    def leave(pair):
+        ends = pl.ds(pair * 2 * CAP, 2 * CAP)
+        return pltpu.make_async_copy(made.at[ends], out_ref.at[ends], gone.at[pair])
 
     def deal(*totals):
         for pair in range(owners // 2):
@@ -327,7 +332,7 @@
             pltpu.matmul_push_rhs(
                 jnp.concatenate(sides, axis=1), pair // 2 % 2, pair % 2, transpose=True
             )
-            pltpu.matmul_acc_lhs(total, turn, load_staged_rhs=pair // 2 % 2)
+            pltpu.matmul_acc_lhs(total, turn_ref[...], load_staged_rhs=pair // 2 % 2)
             dealt = pltpu.matmul_pop(total)
             for side in range(2):
                 owner = 2 * pair + side
@@ -344,11 +349,14 @@
                         axis=1,
                     )
                     target = (owner // columns * CAP + slot) * columns + owner % columns
-                    out_ref[target] = value.astype(jnp.bfloat16)
+                    made[target] = value.astype(jnp.bfloat16)
+            leave(pair).start()
 
     pl.run_scoped(
         deal, *(pltpu.ACC(mxu_id=index % 2)((2 * LANES, MXU), jnp.float32) for index in range(4))
     )
+    for pair in range(owners // 2):
+        leave(pair).wait()
 
 
 def spectra(segments, volts, taps, owner_map, owners, columns):
@@ -366,19 +374,22 @@
         functools.partial(spectra_kernel, segments, channels, owners, columns, inputs, rows),
         out_shape=jax.ShapeDtypeStruct((owners * CAP, inputs // 2, 4 * count), jnp.bfloat16),
         in_specs=[hbm] * 4,
-        out_specs=pl.BlockSpec(memory_space=pltpu.VMEM),
+        out_specs=hbm,
         scratch_shapes=[
             pltpu.VMEM((blocks, inputs * 2, BLOCK * NFFT), jnp.bfloat16),
             pltpu.VMEM((TAPS * halves, 2 * NFFT), jnp.bfloat16),
             pltpu.VMEM((2 * blocks + LAG, TAPS * halves, LANES), jnp.float32),
             pltpu.VMEM((channels * stride, LANES), jnp.float32),
+            pltpu.VMEM((2 * LANES, MXU), jnp.bfloat16),
             pltpu.VMEM(taps.shape, jnp.float32),
             pltpu.VMEM(trig.shape, jnp.float32),
             pltpu.SMEM((channels,), jnp.int32),
             pltpu.SMEM((owners,), jnp.int32),
             pltpu.SMEM((owners * CAP + 1,), jnp.int32),
+            pltpu.VMEM((owners * CAP, inputs // 2, 4 * count), jnp.bfloat16),
             pltpu.SemaphoreType.DMA((blocks,)),
             pltpu.SemaphoreType.DMA((3,)),
+            pltpu.SemaphoreType.DMA((owners // 2,)),
         ],
         compiler_params=pltpu.CompilerParams(vmem_limit_bytes=48 * 1024 * 1024),
         cost_estimate=pl.CostEstimate(
@@ -451,6 +462,13 @@
             source.at[step], out_hbm.at[target, :, :, step * MXU:(step + 1) * MXU], sem.at[number]
         )
 
+    def copy_part(step, unit):
+        return pltpu.make_async_copy(
+            made.at[step, unit],
+            out_hbm.at[slot, unit, :, step * MXU:(step + 1) * MXU],
+            sem.at[steps + 2 * step + unit],
+        )
+
     if not mine:
         for step in range(steps):
             copy(ready, my_row, step, step).start()
@@ -481,8 +499,8 @@
             for unit in range(2):
                 value = pltpu.matmul_pop(totals[2 * unit + step % 2]) * factor
                 made[step, unit] = value.astype(jnp.bfloat16)
-            if not mine:
-                copy(made, slot, step, steps + step).start()
+                if not mine:
+                    copy_part(step, unit).start()
 
         for step in range(steps):
             for turn, (cols, lead) in enumerate(((cols_a, lead_a), (cols_b, lead_b))):
@@ -504,7 +522,8 @@
     else:
         for step in range(steps):
             copy(ready, my_row, step, step).wait()
-            copy(made, slot, step, steps + step).wait()
+            for unit in range(2):
+                copy_part(step, unit).wait()
 
 
 def visibility(scale, owner_map, cols_a, cols_b, row_count, far=None, ready=None):
@@ -514,7 +533,7 @@
     hbm = pl.BlockSpec(memory_space=pltpu.HBM)
     kept = (steps, 2, row_count, MXU)
     scratch = [pltpu.VMEM((2, row_count, MXU), jnp.bfloat16)] * 2
-    scratch.append(pltpu.SemaphoreType.DMA((2 * steps,)))
+    scratch.append(pltpu.SemaphoreType.DMA((3 * steps,)))
     if ready is None:
         more, more_spec = (far,), [hbm]
         out_shape = [jax.ShapeDtypeStruct(shape, jnp.bfloat16) for shape in (kept, (total, width))]
@@ -572,7 +591,7 @@
     rows = volts.shape[3] // NFFT
     return (
         4 * volts.shape[1] == LANES
-        and mesh.shape["row"] == CAP == 2
+        and mesh.shape["row"] == mesh.shape["col"] == CAP == 2
         and rows - TAPS + 1 == 6 * UNIT
         and owner_map.shape[0] % 8 == 0
         and TAPS * 2 * owner_map.shape[0] <= 384

time: 51.5 us -> 51.4 us (level)
  no operation moved by 1% of the time
where the time goes in v1:
time: 51.4 us; the launch traced here: 51 us
  Pallas kernels  23.8 us (46%)
  waiting for transfers between devices  14.9 us (29%)
  starting transfers between devices  11.5 us (22%)
    pallas_call x2, Pallas kernels, spectra(): pl.pallas_call(functools.partial(spectra_kernel, segments, channels, owne...  17.5 us
    all_to_all x2, waiting for transfers between devices, tiled_shards(): lax.all_to_all(sent, ('chan', 'row', 'col'), split_axis=0, concat_axis=0,...  14.9 us
    all_to_all x2, starting transfers between devices, tiled_shards(): lax.all_to_all(sent, ('chan', 'row', 'col'), split_axis=0, concat_axis=0,...  10.4 us
    pallas_call x2, Pallas kernels, visibility(): pl.pallas_call(functools.partial(visibility_kernel, scale, ready is None,...  4.88 us
    pallas_call x2, Pallas kernels, order(): pl.pallas_call(order_kernel, out_shape=jax.ShapeDtypeStruct((2 * half, MX...  1.41 us
    ppermute x2, starting transfers between devices, tiled_shards(): other.append(lax.ppermute(own[-1], 'row', swap))  1.07 us
  transfers between devices with their start and end apart: 4, of which 2 were waited for; matrix products, arithmetic and copies ran while one was open for 1% of the time, Pallas kernels for 24%

profile of v1, /device:TPU:0, one launch (start us, length us, event | category | flops | bytes accessed | tf_op | source)
XLA Modules:
  0.0 51.0 jit_solution(4531383395877036961)
XLA Ops:
  0.0 8.7 %spectra.2 = bf16[32,16,384]{2,1,0:T(8,128)(2,1)} custom-call(s32[24]{0:T(128)} %owner_ref.3, bf16[2,32,2,52736]{3,2,1,0:T(2,128)(2,1)} %volts_ref.3, f32[8,512]{1,0:T(8,128)} %taps_hbm.3, f32[48,512]{1,0:T(8,128)} %constant.20.clone.trig_hbm), custom_call_target="tpu_custom_call" | custom-call | flops 5234491392 | bytes 6815744 | tf_op jit(solution)/shard_map/spectra/pallas_call | solution.py:373
  8.7 7.3 %all-to-all-start = ((bf16[32,16,384]{2,1,0:T(8,128)(2,1)}), bf16[32,16,384]{2,1,0:T(8,128)(2,1)S(1)}, u32[]{:S(2)}, u32[]{:S(2)}) async-start(bf16[32,16,384]{2,1,0:T(8,128)(2,1)} %spectra.2), calls=%async_computation | async-start | bytes 786432 | tf_op jit(solution)/shard_map/all_to_all | solution.py:581
  16.1 0.0 copy-start.1
  16.1 8.8 %spectra.3 = bf16[32,16,384]{2,1,0:T(8,128)(2,1)} custom-call(s32[24]{0:T(128)} %owner_ref.3, bf16[2,32,2,52736]{3,2,1,0:T(2,128)(2,1)} %volts_ref.3, f32[8,512]{1,0:T(8,128)} %taps_hbm.3, f32[48,512]{1,0:T(8,128)} %constant.20.clone.trig_hbm), custom_call_target="tpu_custom_call" | custom-call | flops 5234491392 | bytes 6815744 | tf_op jit(solution)/shard_map/spectra/pallas_call | solution.py:373
  24.8 4.0 %all-to-all-done = bf16[32,16,384]{2,1,0:T(8,128)(2,1)S(1)} async-done(((bf16[32,16,384]{2,1,0:T(8,128)(2,1)}), bf16[32,16,384]{2,1,0:T(8,128)(2,1)S(1)}, u32[]{:S(2)}, u32[]{:S(2)}) %all-to-all-start) | async-done | bytes 393248 | tf_op jit(solution)/shard_map/all_to_all | solution.py:581
  28.8 3.1 %all-to-all-start.1 = ((bf16[32,16,384]{2,1,0:T(8,128)(2,1)}), bf16[32,16,384]{2,1,0:T(8,128)(2,1)S(1)}, u32[]{:S(2)}, u32[]{:S(2)}) async-start(bf16[32,16,384]{2,1,0:T(8,128)(2,1)} %spectra.3), calls=%async_computation.1 | async-start | bytes 786432 | tf_op jit(solution)/shard_map/all_to_all | solution.py:581
  31.9 0.0 copy-done.1
  31.9 0.1 broadcast_in_dim.2
  32.0 0.0 copy-start
  32.0 0.2 reshape.24
  32.2 0.4 fusion.place_ref
  32.6 0.7 %order.2.cols_a = bf16[1024,256]{1,0:T(8,128)(2,1)S(1)} custom-call(bf16[1024,1024]{1,0:T(8,128)(2,1)S(1)} %fusion.place_ref, bf16[512,384]{1,0:T(8,128)(2,1)S(1)} %bitcast.2), custom_call_target="tpu_custom_call" | custom-call | flops 536870912 | bytes 2097152 | tf_op jit(solution)/shard_map/order/pallas_call | solution.py:435
  33.3 0.3 collective-permute-start
  33.6 11.0 %all-to-all-done.1 = bf16[32,16,384]{2,1,0:T(8,128)(2,1)S(1)} async-done(((bf16[32,16,384]{2,1,0:T(8,128)(2,1)}), bf16[32,16,384]{2,1,0:T(8,128)(2,1)S(1)}, u32[]{:S(2)}, u32[]{:S(2)}) %all-to-all-start.1) | async-done | bytes 393248 | tf_op jit(solution)/shard_map/all_to_all | solution.py:581
  44.6 0.7 %order.3.cols_b = bf16[1024,256]{1,0:T(8,128)(2,1)S(1)} custom-call(bf16[1024,1024]{1,0:T(8,128)(2,1)S(1)} %fusion.place_ref, bf16[512,384]{1,0:T(8,128)(2,1)S(1)} %bitcast.3), custom_call_target="tpu_custom_call" | custom-call | flops 536870912 | bytes 2097152 | tf_op jit(solution)/shard_map/order/pallas_call | solution.py:435
  45.3 0.8 %collective-permute-start.1 = (bf16[1024,256]{1,0:T(8,128)(2,1)S(1)}, bf16[1024,256]{1,0:T(8,128)(2,1)S(1)}, u32[]{:S(2)}, u32[]{:S(2)}) collective-permute-start(bf16[1024,256]{1,0:T(8,128)(2,1)S(1)} %order.3.cols_b), channel_id=1, source_target_pairs={{0,2},{2,0},{1,3},{3,1},{4,6},{6,4},{5,7},{7,5},{8,10},{10,8},{9,1... | collective-permute-start | bytes 1572872 | tf_op jit(solution)/shard_map/ppermute | solution.py:585
  46.1 0.0 collective-permute-done.rest_0_
  46.1 0.0 copy-done
  46.1 2.0 %visibility.2 = (bf16[4,2,512,256]{3,2,1,0:T(8,128)(2,1)S(1)}, bf16[1024,256]{1,0:T(8,128)(2,1)S(1)}) custom-call(s32[24]{0:T(128)S(1)} %copy-done, bf16[1024,256]{1,0:T(8,128)(2,1)S(1)} %order.2.cols_a, bf16[1024,256]{1,0:T(8,128)(2,1)S(1)} %order.3.cols_b, bf16[1024,256]{1,0:T(8,128)(2,1)} %collective-permute-done.rest_0_), custom_call_target="tpu_custom_call" | custom-call | flops 1073741824 | bytes 4194304 | tf_op jit(solution)/shard_map/visibility/pallas_call | solution.py:546
  48.0 0.0 collective-permute-done.1.cols_b
  48.0 2.9 %visibility.3 = bf16[2,2,512,1024]{3,2,1,0:T(8,128)(2,1)} custom-call(s32[24]{0:T(128)S(1)} %copy-done, bf16[1024,256]{1,0:T(8,128)(2,1)S(1)} %get-tuple-element.13.cols_a, bf16[1024,256]{1,0:T(8,128)(2,1)S(1)} %collective-permute-done.1.cols_b, bf16[4,2,512,256]{3,2,1,0:T(8,128)(2,1)S(1)} %get-tuple-element.14.rest_0_), custom_call_target="tpu_custom_call" | custom-call | flops 1073741824 | bytes 4194304 | tf_op jit(solution)/shard_map/visibility/pallas_call | solution.py:546
  (1 shorter events, 0.0 us)
Async XLA Ops:
  8.7 20.1 %all-to-all-start = ((bf16[32,16,384]{2,1,0:T(8,128)(2,1)}), bf16[32,16,384]{2,1,0:T(8,128)(2,1)S(1)}, u32[]{:S(2)}, u32[]{:S(2)}) async-start(bf16[32,16,384]{2,1,0:T(8,128)(2,1)} %spectra.2), calls=%async_computation | async-start | bytes 786432 | tf_op jit(solution)/shard_map/all_to_all | solution.py:581
  16.1 15.8 %copy-start.1 = (s32[512]{0:T(512)S(1)}, s32[512]{0:T(512)}, u32[]{:S(2)}) copy-start(s32[512]{0:T(512)} %param.9) | copy-start | bytes 6148
  28.8 15.8 %all-to-all-start.1 = ((bf16[32,16,384]{2,1,0:T(8,128)(2,1)}), bf16[32,16,384]{2,1,0:T(8,128)(2,1)S(1)}, u32[]{:S(2)}, u32[]{:S(2)}) async-start(bf16[32,16,384]{2,1,0:T(8,128)(2,1)} %spectra.3), calls=%async_computation.1 | async-start | bytes 786432 | tf_op jit(solution)/shard_map/all_to_all | solution.py:581
  32.0 14.1 %copy-start = (s32[24]{0:T(128)S(1)}, s32[24]{0:T(128)}, u32[]{:S(2)}) copy-start(s32[24]{0:T(128)} %owner_ref.3) | copy-start | bytes 292
  33.3 12.7 %collective-permute-start = (bf16[1024,256]{1,0:T(8,128)(2,1)S(1)}, bf16[1024,256]{1,0:T(8,128)(2,1)}, u32[]{:S(2)}, u32[]{:S(2)}) collective-permute-start(bf16[1024,256]{1,0:T(8,128)(2,1)S(1)} %order.2.cols_a), channel_id=1, source_target_pairs={{0,2},{2,0},{1,3},{3,1},{4,6},{6,4},{5,7},{7,5},{8,10},{10,8},{9,1... | collective-permute-start | bytes 1572872 | tf_op jit(solution)/shard_map/ppermute | solution.py:585
  45.3 2.7 %collective-permute-start.1 = (bf16[1024,256]{1,0:T(8,128)(2,1)S(1)}, bf16[1024,256]{1,0:T(8,128)(2,1)S(1)}, u32[]{:S(2)}, u32[]{:S(2)}) collective-permute-start(bf16[1024,256]{1,0:T(8,128)(2,1)S(1)} %order.3.cols_b), channel_id=1, source_target_pairs={{0,2},{2,0},{1,3},{3,1},{4,6},{6,4},{5,7},{7,5},{8,10},{10,8},{9,1... | collective-permute-start | bytes 1572872 | tf_op jit(solution)/shard_map/ppermute | solution.py:585

commit v2 on v1

--- a/solution.py
+++ b/solution.py
@@ -407,26 +407,34 @@
         got_ref[:, LANES:2 * LANES].astype(jnp.float32), LANES - 2 * UNIT, 1
     ).astype(jnp.bfloat16)
 
+    piece = half // 2
+
     def run(*totals):
-        for k in range(total // MXU):
-            at = slice(k * MXU % half, k * MXU % half + MXU)
-            if k * MXU < half:
-                right = got_ref[at, :2 * LANES]
-            else:
-                right = jnp.concatenate([got_ref[at, 2 * LANES:], second[at]], axis=1)
+        for index in range(2):
+            for k in range(total // MXU):
+                at = slice(k * MXU % half, k * MXU % half + MXU)
+                if k * MXU < half:
+                    right = got_ref[at, :2 * LANES]
+                else:
+                    right = jnp.concatenate([got_ref[at, 2 * LANES:], second[at]], axis=1)
+                for unit in range(2):
+                    first = unit * half + index * piece
+                    pltpu.matmul_push_rhs(right, k % 2, unit)
+                    pltpu.matmul_acc_lhs(
+                        totals[2 * unit + index],
+                        place_ref[first:first + piece, k * MXU:(k + 1) * MXU],
+                        load_staged_rhs=k % 2,
+                    )
+        for index in range(2):
             for unit in range(2):
-                pltpu.matmul_push_rhs(right, k % 2, unit)
-                pltpu.matmul_acc_lhs(
-                    totals[unit],
-                    place_ref[unit * half:(unit + 1) * half, k * MXU:(k + 1) * MXU],
-                    load_staged_rhs=k % 2,
-                )
-        for unit in range(2):
-            cols_ref[unit * half:(unit + 1) * half] = pltpu.matmul_pop(totals[unit]).astype(
-                jnp.bfloat16
-            )
-
-    pl.run_scoped(run, *(pltpu.ACC(mxu_id=unit)((half, MXU), jnp.float32) for unit in range(2)))
+                first = unit * half + index * piece
+                cols_ref[first:first + piece] = pltpu.matmul_pop(
+                    totals[2 * unit + index]
+                ).astype(jnp.bfloat16)
+
+    pl.run_scoped(
+        run, *(pltpu.ACC(mxu_id=index // 2)((piece, MXU), jnp.float32) for index in range(4))
+    )
 
 
 def order(place, got):

time: 51.4 us -> 51.4 us (level)
  no operation moved by 1% of the time
where the time goes in v2:
time: 51.4 us; the launch traced here: 51 us
  Pallas kernels  23.8 us (46%)
  waiting for transfers between devices  14.9 us (29%)
  starting transfers between devices  11.5 us (22%)
    pallas_call x2, Pallas kernels, spectra(): pl.pallas_call(functools.partial(spectra_kernel, segments, channels, owne...  17.5 us
    all_to_all x2, waiting for transfers between devices, tiled_shards(): lax.all_to_all(sent, ('chan', 'row', 'col'), split_axis=0, concat_axis=0,...  14.9 us
    all_to_all x2, starting transfers between devices, tiled_shards(): lax.all_to_all(sent, ('chan', 'row', 'col'), split_axis=0, concat_axis=0,...  10.4 us
    pallas_call x2, Pallas kernels, visibility(): pl.pallas_call(functools.partial(visibility_kernel, scale, ready is None,...  4.88 us
    pallas_call x2, Pallas kernels, order(): pl.pallas_call(order_kernel, out_shape=jax.ShapeDtypeStruct((2 * half, MX...  1.42 us
    ppermute x2, starting transfers between devices, tiled_shards(): other.append(lax.ppermute(own[-1], 'row', swap))  1.07 us
  transfers between devices with their start and end apart: 4, of which 2 were waited for; matrix products, arithmetic and copies ran while one was open for 1% of the time, Pallas kernels for 24%

profile of v2, /device:TPU:0, one launch (start us, length us, event | category | flops | bytes accessed | tf_op | source)
XLA Modules:
  0.0 51.0 jit_solution(11861741600333225406)
XLA Ops:
  0.0 8.7 %spectra.2 = bf16[32,16,384]{2,1,0:T(8,128)(2,1)} custom-call(s32[24]{0:T(128)} %owner_ref.3, bf16[2,32,2,52736]{3,2,1,0:T(2,128)(2,1)} %volts_ref.3, f32[8,512]{1,0:T(8,128)} %taps_hbm.3, f32[48,512]{1,0:T(8,128)} %constant.20.clone.trig_hbm), custom_call_target="tpu_custom_call" | custom-call | flops 5234491392 | bytes 6815744 | tf_op jit(solution)/shard_map/spectra/pallas_call | solution.py:373
  8.7 7.3 %all-to-all-start = ((bf16[32,16,384]{2,1,0:T(8,128)(2,1)}), bf16[32,16,384]{2,1,0:T(8,128)(2,1)S(1)}, u32[]{:S(2)}, u32[]{:S(2)}) async-start(bf16[32,16,384]{2,1,0:T(8,128)(2,1)} %spectra.2), calls=%async_computation | async-start | bytes 786432 | tf_op jit(solution)/shard_map/all_to_all | solution.py:589
  16.1 0.0 copy-start.1
  16.1 8.8 %spectra.3 = bf16[32,16,384]{2,1,0:T(8,128)(2,1)} custom-call(s32[24]{0:T(128)} %owner_ref.3, bf16[2,32,2,52736]{3,2,1,0:T(2,128)(2,1)} %volts_ref.3, f32[8,512]{1,0:T(8,128)} %taps_hbm.3, f32[48,512]{1,0:T(8,128)} %constant.20.clone.trig_hbm), custom_call_target="tpu_custom_call" | custom-call | flops 5234491392 | bytes 6815744 | tf_op jit(solution)/shard_map/spectra/pallas_call | solution.py:373
  24.8 4.0 %all-to-all-done = bf16[32,16,384]{2,1,0:T(8,128)(2,1)S(1)} async-done(((bf16[32,16,384]{2,1,0:T(8,128)(2,1)}), bf16[32,16,384]{2,1,0:T(8,128)(2,1)S(1)}, u32[]{:S(2)}, u32[]{:S(2)}) %all-to-all-start) | async-done | bytes 393248 | tf_op jit(solution)/shard_map/all_to_all | solution.py:589
  28.8 3.1 %all-to-all-start.1 = ((bf16[32,16,384]{2,1,0:T(8,128)(2,1)}), bf16[32,16,384]{2,1,0:T(8,128)(2,1)S(1)}, u32[]{:S(2)}, u32[]{:S(2)}) async-start(bf16[32,16,384]{2,1,0:T(8,128)(2,1)} %spectra.3), calls=%async_computation.1 | async-start | bytes 786432 | tf_op jit(solution)/shard_map/all_to_all | solution.py:589
  31.9 0.0 copy-done.1
  31.9 0.1 broadcast_in_dim.2
  32.0 0.0 copy-start
  32.0 0.2 reshape.24
  32.2 0.4 fusion.place_ref
  32.6 0.7 %order.2.cols_a = bf16[1024,256]{1,0:T(8,128)(2,1)S(1)} custom-call(bf16[1024,1024]{1,0:T(8,128)(2,1)S(1)} %fusion.place_ref, bf16[512,384]{1,0:T(8,128)(2,1)S(1)} %bitcast.2), custom_call_target="tpu_custom_call" | custom-call | flops 536870912 | bytes 2097152 | tf_op jit(solution)/shard_map/order/pallas_call | solution.py:443
  33.3 0.3 collective-permute-start
  33.6 11.0 %all-to-all-done.1 = bf16[32,16,384]{2,1,0:T(8,128)(2,1)S(1)} async-done(((bf16[32,16,384]{2,1,0:T(8,128)(2,1)}), bf16[32,16,384]{2,1,0:T(8,128)(2,1)S(1)}, u32[]{:S(2)}, u32[]{:S(2)}) %all-to-all-start.1) | async-done | bytes 393248 | tf_op jit(solution)/shard_map/all_to_all | solution.py:589
  44.6 0.7 %order.3.cols_b = bf16[1024,256]{1,0:T(8,128)(2,1)S(1)} custom-call(bf16[1024,1024]{1,0:T(8,128)(2,1)S(1)} %fusion.place_ref, bf16[512,384]{1,0:T(8,128)(2,1)S(1)} %bitcast.3), custom_call_target="tpu_custom_call" | custom-call | flops 536870912 | bytes 2097152 | tf_op jit(solution)/shard_map/order/pallas_call | solution.py:443
  45.3 0.8 %collective-permute-start.1 = (bf16[1024,256]{1,0:T(8,128)(2,1)S(1)}, bf16[1024,256]{1,0:T(8,128)(2,1)S(1)}, u32[]{:S(2)}, u32[]{:S(2)}) collective-permute-start(bf16[1024,256]{1,0:T(8,128)(2,1)S(1)} %order.3.cols_b), channel_id=1, source_target_pairs={{0,2},{2,0},{1,3},{3,1},{4,6},{6,4},{5,7},{7,5},{8,10},{10,8},{9,1... | collective-permute-start | bytes 1572872 | tf_op jit(solution)/shard_map/ppermute | solution.py:593
  46.1 0.0 collective-permute-done.rest_0_
  46.1 0.0 copy-done
  46.1 2.0 %visibility.2 = (bf16[4,2,512,256]{3,2,1,0:T(8,128)(2,1)S(1)}, bf16[1024,256]{1,0:T(8,128)(2,1)S(1)}) custom-call(s32[24]{0:T(128)S(1)} %copy-done, bf16[1024,256]{1,0:T(8,128)(2,1)S(1)} %order.2.cols_a, bf16[1024,256]{1,0:T(8,128)(2,1)S(1)} %order.3.cols_b, bf16[1024,256]{1,0:T(8,128)(2,1)} %collective-permute-done.rest_0_), custom_call_target="tpu_custom_call" | custom-call | flops 1073741824 | bytes 4194304 | tf_op jit(solution)/shard_map/visibility/pallas_call | solution.py:554
  48.0 0.0 collective-permute-done.1.cols_b
  48.1 2.9 %visibility.3 = bf16[2,2,512,1024]{3,2,1,0:T(8,128)(2,1)} custom-call(s32[24]{0:T(128)S(1)} %copy-done, bf16[1024,256]{1,0:T(8,128)(2,1)S(1)} %get-tuple-element.13.cols_a, bf16[1024,256]{1,0:T(8,128)(2,1)S(1)} %collective-permute-done.1.cols_b, bf16[4,2,512,256]{3,2,1,0:T(8,128)(2,1)S(1)} %get-tuple-element.14.rest_0_), custom_call_target="tpu_custom_call" | custom-call | flops 1073741824 | bytes 4194304 | tf_op jit(solution)/shard_map/visibility/pallas_call | solution.py:554
  (1 shorter events, 0.0 us)
Async XLA Ops:
  8.7 20.1 %all-to-all-start = ((bf16[32,16,384]{2,1,0:T(8,128)(2,1)}), bf16[32,16,384]{2,1,0:T(8,128)(2,1)S(1)}, u32[]{:S(2)}, u32[]{:S(2)}) async-start(bf16[32,16,384]{2,1,0:T(8,128)(2,1)} %spectra.2), calls=%async_computation | async-start | bytes 786432 | tf_op jit(solution)/shard_map/all_to_all | solution.py:589
  16.1 15.8 %copy-start.1 = (s32[512]{0:T(512)S(1)}, s32[512]{0:T(512)}, u32[]{:S(2)}) copy-start(s32[512]{0:T(512)} %param.9) | copy-start | bytes 6148
  28.8 15.8 %all-to-all-start.1 = ((bf16[32,16,384]{2,1,0:T(8,128)(2,1)}), bf16[32,16,384]{2,1,0:T(8,128)(2,1)S(1)}, u32[]{:S(2)}, u32[]{:S(2)}) async-start(bf16[32,16,384]{2,1,0:T(8,128)(2,1)} %spectra.3), calls=%async_computation.1 | async-start | bytes 786432 | tf_op jit(solution)/shard_map/all_to_all | solution.py:589
  32.0 14.1 %copy-start = (s32[24]{0:T(128)S(1)}, s32[24]{0:T(128)}, u32[]{:S(2)}) copy-start(s32[24]{0:T(128)} %owner_ref.3) | copy-start | bytes 292
  33.3 12.7 %collective-permute-start = (bf16[1024,256]{1,0:T(8,128)(2,1)S(1)}, bf16[1024,256]{1,0:T(8,128)(2,1)}, u32[]{:S(2)}, u32[]{:S(2)}) collective-permute-start(bf16[1024,256]{1,0:T(8,128)(2,1)S(1)} %order.2.cols_a), channel_id=1, source_target_pairs={{0,2},{2,0},{1,3},{3,1},{4,6},{6,4},{5,7},{7,5},{8,10},{10,8},{9,1... | collective-permute-start | bytes 1572872 | tf_op jit(solution)/shard_map/ppermute | solution.py:593
  45.3 2.7 %collective-permute-start.1 = (bf16[1024,256]{1,0:T(8,128)(2,1)S(1)}, bf16[1024,256]{1,0:T(8,128)(2,1)S(1)}, u32[]{:S(2)}, u32[]{:S(2)}) collective-permute-start(bf16[1024,256]{1,0:T(8,128)(2,1)S(1)} %order.3.cols_b), channel_id=1, source_target_pairs={{0,2},{2,0},{1,3},{3,1},{4,6},{6,4},{5,7},{7,5},{8,10},{10,8},{9,1... | collective-permute-start | bytes 1572872 | tf_op jit(solution)/shard_map/ppermute | solution.py:593
